TPU v7x, 32 devices: a whole 2x2x4 slice. The times are simulated.
32 devices in a mesh: grp: 2 (over y), ja: 4 (over z), ia: 4 (over x, core).
Axes of the slice: x: 2, y: 2, z: 4, core: 2. Of those that a mesh axis runs over, the one named last changes fastest.
Arguments:
- pos_vel: float32 [6, 8192], P(None, ('grp', 'ja')), parts along dimension 1, may hold values from -6 to 6
- acc_jerk: float32 [6, 8192], P(None, ('grp', 'ja')), parts along dimension 1, may hold values from -6 to 6
- mass: float32 [8192], P(('grp', 'ja')), parts along dimension 0, may hold values from 7.324219e-05 to 0.0007324219
- age: float32 [8192], P(('grp', 'ja')), parts along dimension 0, may hold values from 0.125 to 0.5
- active_local: int32 [12288], P(('grp', 'ia')), parts along dimension 0, may hold values from 0 to 1023
- active_owner: int32 [12288], P(('grp', 'ia')), parts along dimension 0, may hold values from 0 to 3
Outputs:
- state: float32 [6, 12288], P(None, ('grp', 'ia')), parts along dimension 1
- forces: float32 [7, 12288], P(None, ('grp', 'ia')), parts along dimension 1
There are 2 independent parts, one for each index of `grp`. A program takes and returns all parts, laid end to end along the dimension named above; each array names one. Nothing has to cross between parts.
All inputs are finite; a program needn't handle non-finite values.
Results may differ from a plain program's by a relative error of at most 0.0003.
Values sent between devices are 32-bit elements; how exact they have to be, the bound alone decides.
No kernel may reach another device: no remote copies, remote signals or barrier semaphores. Data moves between devices by JAX's collectives and lax.ppermute only.
A program may use at most 64 MiB of HBM per device.

v0:
```python
import jax
import jax.numpy as jnp
from jax import lax
from jax.sharding import PartitionSpec as P

soften = 0.0004


def predict(pos_vel, acc_jerk, age):
    position = pos_vel[0:3]
    velocity = pos_vel[3:6]
    accel = acc_jerk[0:3]
    jolt = acc_jerk[3:6]
    step_len = age[None, :]
    new_pos = position + step_len * (velocity + step_len * (accel * 0.5 + step_len * jolt / 6.0))
    new_vel = velocity + step_len * (accel + step_len * jolt * 0.5)
    return jnp.concatenate([new_pos, new_vel], axis=0)


def pair_terms(targets, sources, masses):
    delta_pos = sources[0:3, :, None] - targets[0:3, None, :]
    delta_vel = sources[3:6, :, None] - targets[3:6, None, :]
    dist_sq = jnp.sum(delta_pos * delta_pos, axis=0) + soften
    inverse = lax.rsqrt(dist_sq)
    inv_sq = inverse * inverse
    weighted = masses[:, None] * inverse
    weighted_cube = weighted * inv_sq
    radial = 3.0 * jnp.sum(delta_pos * delta_vel, axis=0) * inv_sq
    accel = jnp.sum(weighted_cube[None] * delta_pos, axis=1)
    jolt = jnp.sum(weighted_cube[None] * (delta_vel - radial[None] * delta_pos), axis=1)
    potential = -jnp.sum(weighted, axis=0)
    return jnp.concatenate([accel, jolt, potential[None]], axis=0)


def block_terms(targets, sources, masses):
    count = targets.shape[1]
    width = min(512, count)
    nblocks = count // width
    src_count = sources.shape[1]
    src_width = min(512, src_count)
    src_blocks = src_count // src_width
    source_pieces = sources.reshape(6, src_blocks, src_width).transpose(1, 0, 2)
    mass_pieces = masses.reshape(src_blocks, src_width)
    pieces = targets.reshape(6, nblocks, width).transpose(1, 0, 2)

    def one_block(piece):

        def accumulate(total, parts):
            return (total + pair_terms(piece, parts[0], parts[1]), None)

        total, unused = lax.scan(
            accumulate, jnp.zeros((7, width), jnp.float32), (source_pieces, mass_pieces)
        )
        return total

    results = lax.map(one_block, pieces)
    return results.transpose(1, 0, 2).reshape(7, count)


def correct(history, forces):
    pred_pos = history[0:3]
    pred_vel = history[3:6]
    old_acc = history[6:9]
    old_jolt = history[9:12]
    step_len = history[12:13]
    new_acc = forces[0:3]
    new_jolt = forces[3:6]
    differ = old_acc - new_acc
    square = step_len * step_len
    cubed = square * step_len
    fourth = square * square
    fifth = fourth * step_len
    second = (-6.0 * differ - step_len * (4.0 * old_jolt + 2.0 * new_jolt)) / square
    third = (12.0 * differ + 6.0 * step_len * (old_jolt + new_jolt)) / cubed
    position = pred_pos + fourth / 24.0 * second + fifth / 120.0 * third
    velocity = pred_vel + cubed / 6.0 * second + fourth / 24.0 * third
    return jnp.concatenate([position, velocity], axis=0)


def local(pos_vel, acc_jerk, mass, age, active_local, active_owner):
    shard_rank = lax.axis_index("ja")
    predicted = predict(pos_vel, acc_jerk, age)
    stacked = jnp.concatenate([predicted, acc_jerk, age[None, :]], axis=0)
    picked = jnp.take(stacked, active_local, axis=1)
    owned = active_owner == shard_rank
    contrib = jnp.where(owned[None, :], picked, 0.0)
    history = lax.psum(contrib, "ja")
    partial_value = block_terms(history[0:6], predicted, mass)
    forces = lax.psum(partial_value, "ja")
    state = correct(history, forces)
    return (state, forces)


def solution(mesh):
    return jax.shard_map(
        local,
        mesh=mesh,
        in_specs=(
            P(None, ("grp", "ja")),
            P(None, ("grp", "ja")),
            P(("grp", "ja")),
            P(("grp", "ja")),
            P(("grp", "ia")),
            P(("grp", "ia")),
        ),
        out_specs=(P(None, ("grp", "ia")), P(None, ("grp", "ia"))),
        check_vma=False,
    )
```

profile of v0, /device:TPU:0, one launch (start us, length us, event | category | flops | bytes accessed | tf_op | source)
XLA Modules:
  0.0 92.8 jit_solution(16712219660879244907)
XLA Ops:
  7.2 0.0 all-reduce.2.cloned.1.call-start
  7.2 0.7 compare_select_fusion
  7.9 0.9 multiply_add_fusion.1
  8.8 0.8 pad_maximum_fusion
  9.6 0.0 copy-start.2
  9.6 0.0 copy-start.3
  9.6 0.2 copy.93
  9.8 0.0 copy-start.4
  9.9 2.6 %gather_fusion = f32[1536,13]{1,0:T(8,128)S(1)} fusion(f32[13,1024]{0,1:T(8,128)S(1)} %copy.93, s32[2048]{0:T(1024)S(1)} %pad_clamp_fusion), kind=kCustom, calls=%fused_computation | custom fusion | bytes 165888 | tf_op jit(solution)/shard_map/jit(_take)/gather | solution.py:84
  12.5 0.3 copy.94
  12.7 0.0 copy-done.2
  12.7 0.0 copy-done.3
  12.8 0.7 select_bitcast_fusion
  13.4 0.0 all-reduce.2.cloned.1.call-update
  13.4 0.0 copy-done.4
  13.5 37.3 %all-reduce.2.cloned.1.call-done = f32[13,1536]{1,0:T(8,128)} async-done(((f32[13,1536]{1,0:T(8,128)}), f32[13,1536]{1,0:T(8,128)}) %all-reduce.2.cloned.1.call-update) | async-done | bytes 79888 | tf_op jit(solution)/shard_map/psum | solution.py:87
  50.8 0.8 slice.71
  51.6 0.0 copy-start
  51.6 15.3 %while.22 = (s32[]{:T(128)}, f32[3,7,512]{2,1,0:T(8,128)S(1)}, f32[3,6,512]{2,1,0:T(8,128)S(1)}, f32[2,512]{1,0:T(2,128)S(1)}, f32[2,6,512]{2,1,0:T(8,128)S(1)},...) while((s32[]{:T(128)}, f32[3,7,512]{2,1,0:T(8,128)S(1)}, f32[3,6,512]{2,1,0:T(8,128)S(1)}, ...), condition=%wide.region_9.10_spmd, body=%wide.region_1.9_spmd.sunk | while | flops 12332038 | bytes 8612156 | solution.py:56
  51.6 5.1 %while.23 = (s32[]{:T(128)}, f32[7,512]{1,0:T(8,128)S(1)}, f32[2,512]{1,0:T(2,128)S(1)}, f32[2,6,512]{2,1,0:T(8,128)S(1)}, f32[6,512]{1,0:T(8,128)S(1)}, /*index=5*/s32[]{:T(128)}, s32[]{:T(128)}, s32[]{}) while((s32[]{:T(128)}, f32[7,512]{1,0:T(8,128)S(1)}, f32[2,512]{1,0:T(2,128)S(1)}, f32[2,6,512]{2,1,0:T(8,128)S(1)}, ...), condition=%wide.region_8.8_spmd.clone, body=%wide.region_2.7_spmd.clone.sunk | while | flops 12332036 | bytes 8554623 | solution.py:51
  51.7 1.0 %fusion.13 = (f32[512,512]{1,0:T(8,128)S(1)}, f32[512,512]{1,0:T(8,128)S(1)}) fusion(f32[3,512]{1,0:T(4,128)S(1)} %get-tuple-element.214, f32[3,512]{1,0:T(4,128)S(1)} %get-tuple-element.215, f32[3,512]{1,0:T(4,128)S(1)} %get-tuple-element.216, f32[3,512]{1,0:T(4,128)S(1)} %get-tuple-element.217), kind=kLoop, calls=%fused_computation.10.clone.1 | loop fusion | flops 4194304 | bytes 2121728 | tf_op jit(solution)/shard_map/while/body/eval_jaxpr/while/body/eval_jaxpr/reduce_sum | solution.py:28
  52.6 0.3 multiply_multiply_fusion.5
  53.0 1.1 %fusion.14 = (f32[3,512]{1,0:T(4,128)S(1)}, f32[3,512]{1,0:T(4,128)S(1)}) fusion(f32[512,512]{1,0:T(8,128)S(1)} %get-tuple-element.221, f32[3,512]{1,0:T(4,128)S(1)} %get-tuple-element.216, f32[3,512]{1,0:T(4,128)S(1)} %get-tuple-element.217, f32[512,512]{1,0:T(8,128)S(1)} %get-tuple-element.222, f32[3,512]{1,0:T(4,128)S(1)} %get-tuple-element.214, ...), kind=kLoop, calls=%fused_computation.9.clone.1 | loop fusion | flops 6288384 | bytes 2134016 | tf_op jit(solution)/shard_map/while/body/eval_jaxpr/while/body/eval_jaxpr/reduce_sum | solution.py:29
  54.2 1.0 %fusion.13 = (f32[512,512]{1,0:T(8,128)S(1)}, f32[512,512]{1,0:T(8,128)S(1)}) fusion(f32[3,512]{1,0:T(4,128)S(1)} %get-tuple-element.214, f32[3,512]{1,0:T(4,128)S(1)} %get-tuple-element.215, f32[3,512]{1,0:T(4,128)S(1)} %get-tuple-element.216, f32[3,512]{1,0:T(4,128)S(1)} %get-tuple-element.217), kind=kLoop, calls=%fused_computation.10.clone.1 | loop fusion | flops 4194304 | bytes 2121728 | tf_op jit(solution)/shard_map/while/body/eval_jaxpr/while/body/eval_jaxpr/reduce_sum | solution.py:28
  55.2 0.3 multiply_multiply_fusion.5
  55.5 1.1 %fusion.14 = (f32[3,512]{1,0:T(4,128)S(1)}, f32[3,512]{1,0:T(4,128)S(1)}) fusion(f32[512,512]{1,0:T(8,128)S(1)} %get-tuple-element.221, f32[3,512]{1,0:T(4,128)S(1)} %get-tuple-element.216, f32[3,512]{1,0:T(4,128)S(1)} %get-tuple-element.217, f32[512,512]{1,0:T(8,128)S(1)} %get-tuple-element.222, f32[3,512]{1,0:T(4,128)S(1)} %get-tuple-element.214, ...), kind=kLoop, calls=%fused_computation.9.clone.1 | loop fusion | flops 6288384 | bytes 2134016 | tf_op jit(solution)/shard_map/while/body/eval_jaxpr/while/body/eval_jaxpr/reduce_sum | solution.py:29
  56.7 5.1 %while.23 = (s32[]{:T(128)}, f32[7,512]{1,0:T(8,128)S(1)}, f32[2,512]{1,0:T(2,128)S(1)}, f32[2,6,512]{2,1,0:T(8,128)S(1)}, f32[6,512]{1,0:T(8,128)S(1)}, /*index=5*/s32[]{:T(128)}, s32[]{:T(128)}, s32[]{}) while((s32[]{:T(128)}, f32[7,512]{1,0:T(8,128)S(1)}, f32[2,512]{1,0:T(2,128)S(1)}, f32[2,6,512]{2,1,0:T(8,128)S(1)}, ...), condition=%wide.region_8.8_spmd.clone, body=%wide.region_2.7_spmd.clone.sunk | while | flops 12332036 | bytes 8554623 | solution.py:51
  56.8 1.0 %fusion.13 = (f32[512,512]{1,0:T(8,128)S(1)}, f32[512,512]{1,0:T(8,128)S(1)}) fusion(f32[3,512]{1,0:T(4,128)S(1)} %get-tuple-element.214, f32[3,512]{1,0:T(4,128)S(1)} %get-tuple-element.215, f32[3,512]{1,0:T(4,128)S(1)} %get-tuple-element.216, f32[3,512]{1,0:T(4,128)S(1)} %get-tuple-element.217), kind=kLoop, calls=%fused_computation.10.clone.1 | loop fusion | flops 4194304 | bytes 2121728 | tf_op jit(solution)/shard_map/while/body/eval_jaxpr/while/body/eval_jaxpr/reduce_sum | solution.py:28
  57.8 0.3 multiply_multiply_fusion.5
  58.1 1.1 %fusion.14 = (f32[3,512]{1,0:T(4,128)S(1)}, f32[3,512]{1,0:T(4,128)S(1)}) fusion(f32[512,512]{1,0:T(8,128)S(1)} %get-tuple-element.221, f32[3,512]{1,0:T(4,128)S(1)} %get-tuple-element.216, f32[3,512]{1,0:T(4,128)S(1)} %get-tuple-element.217, f32[512,512]{1,0:T(8,128)S(1)} %get-tuple-element.222, f32[3,512]{1,0:T(4,128)S(1)} %get-tuple-element.214, ...), kind=kLoop, calls=%fused_computation.9.clone.1 | loop fusion | flops 6288384 | bytes 2134016 | tf_op jit(solution)/shard_map/while/body/eval_jaxpr/while/body/eval_jaxpr/reduce_sum | solution.py:29
  59.3 1.0 %fusion.13 = (f32[512,512]{1,0:T(8,128)S(1)}, f32[512,512]{1,0:T(8,128)S(1)}) fusion(f32[3,512]{1,0:T(4,128)S(1)} %get-tuple-element.214, f32[3,512]{1,0:T(4,128)S(1)} %get-tuple-element.215, f32[3,512]{1,0:T(4,128)S(1)} %get-tuple-element.216, f32[3,512]{1,0:T(4,128)S(1)} %get-tuple-element.217), kind=kLoop, calls=%fused_computation.10.clone.1 | loop fusion | flops 4194304 | bytes 2121728 | tf_op jit(solution)/shard_map/while/body/eval_jaxpr/while/body/eval_jaxpr/reduce_sum | solution.py:28
  60.3 0.3 multiply_multiply_fusion.5
  60.6 1.1 %fusion.14 = (f32[3,512]{1,0:T(4,128)S(1)}, f32[3,512]{1,0:T(4,128)S(1)}) fusion(f32[512,512]{1,0:T(8,128)S(1)} %get-tuple-element.221, f32[3,512]{1,0:T(4,128)S(1)} %get-tuple-element.216, f32[3,512]{1,0:T(4,128)S(1)} %get-tuple-element.217, f32[512,512]{1,0:T(8,128)S(1)} %get-tuple-element.222, f32[3,512]{1,0:T(4,128)S(1)} %get-tuple-element.214, ...), kind=kLoop, calls=%fused_computation.9.clone.1 | loop fusion | flops 6288384 | bytes 2134016 | tf_op jit(solution)/shard_map/while/body/eval_jaxpr/while/body/eval_jaxpr/reduce_sum | solution.py:29
  61.8 5.1 %while.23 = (s32[]{:T(128)}, f32[7,512]{1,0:T(8,128)S(1)}, f32[2,512]{1,0:T(2,128)S(1)}, f32[2,6,512]{2,1,0:T(8,128)S(1)}, f32[6,512]{1,0:T(8,128)S(1)}, /*index=5*/s32[]{:T(128)}, s32[]{:T(128)}, s32[]{}) while((s32[]{:T(128)}, f32[7,512]{1,0:T(8,128)S(1)}, f32[2,512]{1,0:T(2,128)S(1)}, f32[2,6,512]{2,1,0:T(8,128)S(1)}, ...), condition=%wide.region_8.8_spmd.clone, body=%wide.region_2.7_spmd.clone.sunk | while | flops 12332036 | bytes 8554623 | solution.py:51
  61.9 1.0 %fusion.13 = (f32[512,512]{1,0:T(8,128)S(1)}, f32[512,512]{1,0:T(8,128)S(1)}) fusion(f32[3,512]{1,0:T(4,128)S(1)} %get-tuple-element.214, f32[3,512]{1,0:T(4,128)S(1)} %get-tuple-element.215, f32[3,512]{1,0:T(4,128)S(1)} %get-tuple-element.216, f32[3,512]{1,0:T(4,128)S(1)} %get-tuple-element.217), kind=kLoop, calls=%fused_computation.10.clone.1 | loop fusion | flops 4194304 | bytes 2121728 | tf_op jit(solution)/shard_map/while/body/eval_jaxpr/while/body/eval_jaxpr/reduce_sum | solution.py:28
  62.9 0.3 multiply_multiply_fusion.5
  63.2 1.1 %fusion.14 = (f32[3,512]{1,0:T(4,128)S(1)}, f32[3,512]{1,0:T(4,128)S(1)}) fusion(f32[512,512]{1,0:T(8,128)S(1)} %get-tuple-element.221, f32[3,512]{1,0:T(4,128)S(1)} %get-tuple-element.216, f32[3,512]{1,0:T(4,128)S(1)} %get-tuple-element.217, f32[512,512]{1,0:T(8,128)S(1)} %get-tuple-element.222, f32[3,512]{1,0:T(4,128)S(1)} %get-tuple-element.214, ...), kind=kLoop, calls=%fused_computation.9.clone.1 | loop fusion | flops 6288384 | bytes 2134016 | tf_op jit(solution)/shard_map/while/body/eval_jaxpr/while/body/eval_jaxpr/reduce_sum | solution.py:29
  64.4 1.0 %fusion.13 = (f32[512,512]{1,0:T(8,128)S(1)}, f32[512,512]{1,0:T(8,128)S(1)}) fusion(f32[3,512]{1,0:T(4,128)S(1)} %get-tuple-element.214, f32[3,512]{1,0:T(4,128)S(1)} %get-tuple-element.215, f32[3,512]{1,0:T(4,128)S(1)} %get-tuple-element.216, f32[3,512]{1,0:T(4,128)S(1)} %get-tuple-element.217), kind=kLoop, calls=%fused_computation.10.clone.1 | loop fusion | flops 4194304 | bytes 2121728 | tf_op jit(solution)/shard_map/while/body/eval_jaxpr/while/body/eval_jaxpr/reduce_sum | solution.py:28
  65.4 0.3 multiply_multiply_fusion.5
  65.7 1.1 %fusion.14 = (f32[3,512]{1,0:T(4,128)S(1)}, f32[3,512]{1,0:T(4,128)S(1)}) fusion(f32[512,512]{1,0:T(8,128)S(1)} %get-tuple-element.221, f32[3,512]{1,0:T(4,128)S(1)} %get-tuple-element.216, f32[3,512]{1,0:T(4,128)S(1)} %get-tuple-element.217, f32[512,512]{1,0:T(8,128)S(1)} %get-tuple-element.222, f32[3,512]{1,0:T(4,128)S(1)} %get-tuple-element.214, ...), kind=kLoop, calls=%fused_computation.9.clone.1 | loop fusion | flops 6288384 | bytes 2134016 | tf_op jit(solution)/shard_map/while/body/eval_jaxpr/while/body/eval_jaxpr/reduce_sum | solution.py:29
  66.9 18.2 %psum.15 = f32[7,1536]{1,0:T(8,128)S(1)} all-reduce(f32[7,1536]{1,0:T(8,128)S(1)} %bitcast.36), channel_id=1, replica_groups=mesh['grp'=2,'ja'=4,'ia'=4] {'ja'}, use_global_device_ids=true, to_apply=%region_10.11 | all-reduce | flops 10752 | bytes 86016 | tf_op jit(solution)/shard_map/psum | solution.py:89
  85.1 0.0 copy-done
  85.1 0.0 copy-start.1
  85.1 0.1 multiply_reduce_fusion.3
  85.2 0.1 fusion.6
  85.3 0.6 pad_maximum_fusion.1
  86.0 0.0 copy-done.1
  (45 shorter events, 0.4 us)
Async XLA Ops:
  7.2 43.6 %all-reduce.2.cloned.1.call-start = ((), (), s32[]{:S(2)}) async-start(), calls=%async_computation | async-start | bytes 196608 | tf_op jit(solution)/shard_map/psum | solution.py:87
  9.6 3.1 %copy-start.2 = (s32[1536]{0:T(1024)S(1)}, s32[1536]{0:T(1024)}, u32[]{:S(2)}) copy-start(s32[1536]{0:T(1024)} %param.14) | copy-start | bytes 18436
  9.6 3.1 %copy-start.3 = (s32[1536]{0:T(1024)S(1)}, s32[1536]{0:T(1024)}, u32[]{:S(2)}) copy-start(s32[1536]{0:T(1024)} %param.15) | copy-start | bytes 18436
  9.8 3.6 %copy-start.4 = (f32[1024]{0:T(1024)S(1)}, f32[1024]{0:T(1024)}, u32[]{:S(2)}) copy-start(f32[1024]{0:T(1024)} %param.12) | copy-start | bytes 12292
  51.6 33.5 %copy-start = (f32[13,1536]{1,0:T(8,128)S(1)}, f32[13,1536]{1,0:T(8,128)}, u32[]{:S(2)}) copy-start(f32[13,1536]{1,0:T(8,128)} %all-reduce.2.cloned.1.call-done) | copy-start | bytes 239620
  85.1 0.9 copy-start.1
Sparse Core Ops, SparseCore 0:
  13.5 37.1 all-reduce.1
where the time goes:
time: 93.2 us; the launch traced here: 92.8 us
  waiting for transfers between devices  37.3 us (40%)
  other arithmetic  18.5 us (20%)
  blocking collectives  18.2 us (20%)
  between operations  14.2 us (15%)
  local copies, waits for them, and re-layouts  4.12 us (4%)
    psum x1, waiting for transfers between devices, local(): history = lax.psum(contrib, 'ja')  37.3 us
    psum x1, blocking collectives, local(): forces = lax.psum(partial_value, 'ja')  18.2 us
    reduce_sum x6, other arithmetic, pair_terms(): accel = jnp.sum(weighted_cube[None] * delta_pos, axis=1)  6.74 us
    reduce_sum x6, other arithmetic, pair_terms(): radial = 3.0 * jnp.sum(delta_pos * delta_vel, axis=0) * inv_sq  5.85 us
    gather x2, local copies, waits for them, and re-layouts, local(): picked = jnp.take(stacked, active_local, axis=1)  2.86 us
  transfers between devices with their start and end apart: 1, of which 1 were waited for; matrix products, arithmetic and copies ran while one was open for 0% of the time, Pallas kernels for 0%

commit v1 on v0

--- a/solution.py
+++ b/solution.py
@@ -2,6 +2,7 @@
 import jax.numpy as jnp
 from jax import lax
 from jax.sharding import PartitionSpec as P
+from jax.lax import axis_size, ppermute
 
 soften = 0.0004
 
@@ -86,7 +87,14 @@
     contrib = jnp.where(owned[None, :], picked, 0.0)
     history = lax.psum(contrib, "ja")
     partial_value = block_terms(history[0:6], predicted, mass)
-    forces = lax.psum(partial_value, "ja")
+    how_many = axis_size("ja")
+    forces, a_next = (partial_value, 0)
+    while 1 << a_next < how_many:
+        finding = ppermute(
+            forces, axis_name="ja", perm=[(s, s ^ 1 << a_next) for s in range(how_many)]
+        )
+        forces = forces + finding
+        a_next = a_next + 1
     state = correct(history, forces)
     return (state, forces)
 

time: 93.2 us -> 84 us (0.901)
  blocking collectives: 18.2 us -> 0 us
  waiting for transfers between devices: 37.3 us -> 42.3 us
  starting transfers between devices: 0.04 us -> 4.1 us
    psum x1 -> x0, blocking collectives: 18.2 us -> none  [local(): forces = lax.psum(partial_value, 'ja')]
    ppermute x0 -> x2, waiting for transfers between devices: none -> 5.02 us  [local(): ppermute(forces, axis_name='ja', perm=[(s, s ^ 1 << a_next) for s in rang...]
    ppermute x0 -> x2, starting transfers between devices: none -> 4.06 us  [local(): ppermute(forces, axis_name='ja', perm=[(s, s ^ 1 << a_next) for s in rang...]
  transfers between devices with their start and end apart: 1 -> 3, of which waited for: 1 -> 3; matrix products, arithmetic and copies ran while one was open for 0% -> 0% of each run, Pallas kernels for 0% -> 0%
where the time goes in v1:
time: 84 us; the launch traced here: 83.7 us
  waiting for transfers between devices  42.3 us (50%)
  other arithmetic  18.4 us (22%)
  between operations  14.1 us (17%)
  local copies, waits for them, and re-layouts  4.12 us (5%)
  starting transfers between devices  4.1 us (5%)
    psum x1, waiting for transfers between devices, local(): history = lax.psum(contrib, 'ja')  37.3 us
    reduce_sum x6, other arithmetic, pair_terms(): accel = jnp.sum(weighted_cube[None] * delta_pos, axis=1)  6.69 us
    reduce_sum x6, other arithmetic, pair_terms(): radial = 3.0 * jnp.sum(delta_pos * delta_vel, axis=0) * inv_sq  5.78 us
    ppermute x2, waiting for transfers between devices, local(): ppermute(forces, axis_name='ja', perm=[(s, s ^ 1 << a_next) for s in rang...  5.02 us
    ppermute x2, starting transfers between devices, local(): ppermute(forces, axis_name='ja', perm=[(s, s ^ 1 << a_next) for s in rang...  4.06 us
    gather x2, local copies, waits for them, and re-layouts, local(): picked = jnp.take(stacked, active_local, axis=1)  2.86 us
    mul x6, other arithmetic, pair_terms(): weighted_cube = weighted * inv_sq  1.86 us
  transfers between devices with their start and end apart: 3, of which 3 were waited for; matrix products, arithmetic and copies ran while one was open for 0% of the time, Pallas kernels for 0%

profile of v1, /device:TPU:0, one launch (start us, length us, event | category | flops | bytes accessed | tf_op | source)
XLA Modules:
  0.0 83.7 jit_solution(17084433539700668973)
XLA Ops:
  7.2 0.0 all-reduce.2.cloned.1.call-start
  7.2 0.9 %multiply_add_fusion.1 = (f32[3,1024]{1,0:T(4,128)S(1)}, f32[3,1024]{1,0:T(4,128)S(1)}) fusion(f32[6,1024]{1,0:T(8,128)} %param.10, f32[6,1024]{1,0:T(8,128)} %param.11, f32[1024]{0:T(1024)} %param.13), kind=kLoop, calls=%fused_computation.34 | loop fusion | flops 36864 | bytes 77824 | tf_op jit(solution)/shard_map/add | solution.py:16
  8.1 0.8 pad_maximum_fusion
  8.9 0.2 copy.101
  9.1 0.0 copy-start.2
  9.1 0.0 copy-start.3
  9.1 0.8 compare_select_fusion
  9.9 0.0 copy-start.4
  9.9 2.6 %gather_fusion = f32[1536,13]{1,0:T(8,128)S(1)} fusion(f32[13,1024]{0,1:T(8,128)S(1)} %copy.101, s32[2048]{0:T(1024)S(1)} %pad_clamp_fusion), kind=kCustom, calls=%fused_computation | custom fusion | bytes 165888 | tf_op jit(solution)/shard_map/jit(_take)/gather | solution.py:85
  12.5 0.3 copy.102
  12.8 0.0 copy-done.2
  12.8 0.0 copy-done.3
  12.8 0.7 select_bitcast_fusion
  13.5 0.0 all-reduce.2.cloned.1.call-update
  13.5 0.0 copy-done.4
  13.5 37.3 %all-reduce.2.cloned.1.call-done = f32[13,1536]{1,0:T(8,128)} async-done(((f32[13,1536]{1,0:T(8,128)}), f32[13,1536]{1,0:T(8,128)}) %all-reduce.2.cloned.1.call-update) | async-done | bytes 79888 | tf_op jit(solution)/shard_map/psum | solution.py:88
  50.8 0.8 slice.71
  51.6 15.2 %while.22 = (s32[]{:T(128)}, f32[3,7,512]{2,1,0:T(8,128)S(1)}, f32[3,6,512]{2,1,0:T(8,128)S(1)}, f32[2,512]{1,0:T(2,128)S(1)}, f32[2,6,512]{2,1,0:T(8,128)S(1)},...) while((s32[]{:T(128)}, f32[3,7,512]{2,1,0:T(8,128)S(1)}, f32[3,6,512]{2,1,0:T(8,128)S(1)}, ...), condition=%wide.region_9.10_spmd, body=%wide.region_1.9_spmd.sunk | while | flops 12332038 | bytes 8612140 | solution.py:57
  51.6 5.0 %while.23 = (s32[]{:T(128)}, f32[7,512]{1,0:T(8,128)S(1)}, f32[2,512]{1,0:T(2,128)S(1)}, f32[2,6,512]{2,1,0:T(8,128)S(1)}, f32[6,512]{1,0:T(8,128)S(1)}, /*index=5*/s32[]{:T(128)}, s32[]{:T(128)}, s32[]{}) while((s32[]{:T(128)}, f32[7,512]{1,0:T(8,128)S(1)}, f32[2,512]{1,0:T(2,128)S(1)}, f32[2,6,512]{2,1,0:T(8,128)S(1)}, ...), condition=%wide.region_8.8_spmd.clone, body=%wide.region_2.7_spmd.clone.sunk | while | flops 12332036 | bytes 8554615 | solution.py:52
  51.7 1.0 %fusion.13 = (f32[512,512]{1,0:T(8,128)S(1)}, f32[512,512]{1,0:T(8,128)S(1)}) fusion(f32[3,512]{1,0:T(4,128)S(1)} %get-tuple-element.214, f32[3,512]{1,0:T(4,128)S(1)} %get-tuple-element.215, f32[3,512]{1,0:T(4,128)S(1)} %get-tuple-element.216, f32[3,512]{1,0:T(4,128)S(1)} %get-tuple-element.217), kind=kLoop, calls=%fused_computation.10.clone.1 | loop fusion | flops 4194304 | bytes 2121728 | tf_op jit(solution)/shard_map/while/body/eval_jaxpr/while/body/eval_jaxpr/reduce_sum | solution.py:29
  52.7 0.3 multiply_multiply_fusion.5
  53.0 1.1 %fusion.14 = (f32[3,512]{1,0:T(4,128)S(1)}, f32[3,512]{1,0:T(4,128)S(1)}) fusion(f32[512,512]{1,0:T(8,128)S(1)} %get-tuple-element.221, f32[3,512]{1,0:T(4,128)S(1)} %get-tuple-element.216, f32[3,512]{1,0:T(4,128)S(1)} %get-tuple-element.217, f32[512,512]{1,0:T(8,128)S(1)} %get-tuple-element.222, f32[3,512]{1,0:T(4,128)S(1)} %get-tuple-element.214, ...), kind=kLoop, calls=%fused_computation.9.clone.1 | loop fusion | flops 6288384 | bytes 2134016 | tf_op jit(solution)/shard_map/while/body/eval_jaxpr/while/body/eval_jaxpr/reduce_sum | solution.py:30
  54.2 1.0 %fusion.13 = (f32[512,512]{1,0:T(8,128)S(1)}, f32[512,512]{1,0:T(8,128)S(1)}) fusion(f32[3,512]{1,0:T(4,128)S(1)} %get-tuple-element.214, f32[3,512]{1,0:T(4,128)S(1)} %get-tuple-element.215, f32[3,512]{1,0:T(4,128)S(1)} %get-tuple-element.216, f32[3,512]{1,0:T(4,128)S(1)} %get-tuple-element.217), kind=kLoop, calls=%fused_computation.10.clone.1 | loop fusion | flops 4194304 | bytes 2121728 | tf_op jit(solution)/shard_map/while/body/eval_jaxpr/while/body/eval_jaxpr/reduce_sum | solution.py:29
  55.2 0.3 multiply_multiply_fusion.5
  55.5 1.1 %fusion.14 = (f32[3,512]{1,0:T(4,128)S(1)}, f32[3,512]{1,0:T(4,128)S(1)}) fusion(f32[512,512]{1,0:T(8,128)S(1)} %get-tuple-element.221, f32[3,512]{1,0:T(4,128)S(1)} %get-tuple-element.216, f32[3,512]{1,0:T(4,128)S(1)} %get-tuple-element.217, f32[512,512]{1,0:T(8,128)S(1)} %get-tuple-element.222, f32[3,512]{1,0:T(4,128)S(1)} %get-tuple-element.214, ...), kind=kLoop, calls=%fused_computation.9.clone.1 | loop fusion | flops 6288384 | bytes 2134016 | tf_op jit(solution)/shard_map/while/body/eval_jaxpr/while/body/eval_jaxpr/reduce_sum | solution.py:30
  56.7 5.0 %while.23 = (s32[]{:T(128)}, f32[7,512]{1,0:T(8,128)S(1)}, f32[2,512]{1,0:T(2,128)S(1)}, f32[2,6,512]{2,1,0:T(8,128)S(1)}, f32[6,512]{1,0:T(8,128)S(1)}, /*index=5*/s32[]{:T(128)}, s32[]{:T(128)}, s32[]{}) while((s32[]{:T(128)}, f32[7,512]{1,0:T(8,128)S(1)}, f32[2,512]{1,0:T(2,128)S(1)}, f32[2,6,512]{2,1,0:T(8,128)S(1)}, ...), condition=%wide.region_8.8_spmd.clone, body=%wide.region_2.7_spmd.clone.sunk | while | flops 12332036 | bytes 8554615 | solution.py:52
  56.8 1.0 %fusion.13 = (f32[512,512]{1,0:T(8,128)S(1)}, f32[512,512]{1,0:T(8,128)S(1)}) fusion(f32[3,512]{1,0:T(4,128)S(1)} %get-tuple-element.214, f32[3,512]{1,0:T(4,128)S(1)} %get-tuple-element.215, f32[3,512]{1,0:T(4,128)S(1)} %get-tuple-element.216, f32[3,512]{1,0:T(4,128)S(1)} %get-tuple-element.217), kind=kLoop, calls=%fused_computation.10.clone.1 | loop fusion | flops 4194304 | bytes 2121728 | tf_op jit(solution)/shard_map/while/body/eval_jaxpr/while/body/eval_jaxpr/reduce_sum | solution.py:29
  57.8 0.3 multiply_multiply_fusion.5
  58.1 1.1 %fusion.14 = (f32[3,512]{1,0:T(4,128)S(1)}, f32[3,512]{1,0:T(4,128)S(1)}) fusion(f32[512,512]{1,0:T(8,128)S(1)} %get-tuple-element.221, f32[3,512]{1,0:T(4,128)S(1)} %get-tuple-element.216, f32[3,512]{1,0:T(4,128)S(1)} %get-tuple-element.217, f32[512,512]{1,0:T(8,128)S(1)} %get-tuple-element.222, f32[3,512]{1,0:T(4,128)S(1)} %get-tuple-element.214, ...), kind=kLoop, calls=%fused_computation.9.clone.1 | loop fusion | flops 6288384 | bytes 2134016 | tf_op jit(solution)/shard_map/while/body/eval_jaxpr/while/body/eval_jaxpr/reduce_sum | solution.py:30
  59.3 1.0 %fusion.13 = (f32[512,512]{1,0:T(8,128)S(1)}, f32[512,512]{1,0:T(8,128)S(1)}) fusion(f32[3,512]{1,0:T(4,128)S(1)} %get-tuple-element.214, f32[3,512]{1,0:T(4,128)S(1)} %get-tuple-element.215, f32[3,512]{1,0:T(4,128)S(1)} %get-tuple-element.216, f32[3,512]{1,0:T(4,128)S(1)} %get-tuple-element.217), kind=kLoop, calls=%fused_computation.10.clone.1 | loop fusion | flops 4194304 | bytes 2121728 | tf_op jit(solution)/shard_map/while/body/eval_jaxpr/while/body/eval_jaxpr/reduce_sum | solution.py:29
  60.3 0.3 multiply_multiply_fusion.5
  60.6 1.1 %fusion.14 = (f32[3,512]{1,0:T(4,128)S(1)}, f32[3,512]{1,0:T(4,128)S(1)}) fusion(f32[512,512]{1,0:T(8,128)S(1)} %get-tuple-element.221, f32[3,512]{1,0:T(4,128)S(1)} %get-tuple-element.216, f32[3,512]{1,0:T(4,128)S(1)} %get-tuple-element.217, f32[512,512]{1,0:T(8,128)S(1)} %get-tuple-element.222, f32[3,512]{1,0:T(4,128)S(1)} %get-tuple-element.214, ...), kind=kLoop, calls=%fused_computation.9.clone.1 | loop fusion | flops 6288384 | bytes 2134016 | tf_op jit(solution)/shard_map/while/body/eval_jaxpr/while/body/eval_jaxpr/reduce_sum | solution.py:30
  61.8 5.0 %while.23 = (s32[]{:T(128)}, f32[7,512]{1,0:T(8,128)S(1)}, f32[2,512]{1,0:T(2,128)S(1)}, f32[2,6,512]{2,1,0:T(8,128)S(1)}, f32[6,512]{1,0:T(8,128)S(1)}, /*index=5*/s32[]{:T(128)}, s32[]{:T(128)}, s32[]{}) while((s32[]{:T(128)}, f32[7,512]{1,0:T(8,128)S(1)}, f32[2,512]{1,0:T(2,128)S(1)}, f32[2,6,512]{2,1,0:T(8,128)S(1)}, ...), condition=%wide.region_8.8_spmd.clone, body=%wide.region_2.7_spmd.clone.sunk | while | flops 12332036 | bytes 8554615 | solution.py:52
  61.9 1.0 %fusion.13 = (f32[512,512]{1,0:T(8,128)S(1)}, f32[512,512]{1,0:T(8,128)S(1)}) fusion(f32[3,512]{1,0:T(4,128)S(1)} %get-tuple-element.214, f32[3,512]{1,0:T(4,128)S(1)} %get-tuple-element.215, f32[3,512]{1,0:T(4,128)S(1)} %get-tuple-element.216, f32[3,512]{1,0:T(4,128)S(1)} %get-tuple-element.217), kind=kLoop, calls=%fused_computation.10.clone.1 | loop fusion | flops 4194304 | bytes 2121728 | tf_op jit(solution)/shard_map/while/body/eval_jaxpr/while/body/eval_jaxpr/reduce_sum | solution.py:29
  62.9 0.3 multiply_multiply_fusion.5
  63.2 1.1 %fusion.14 = (f32[3,512]{1,0:T(4,128)S(1)}, f32[3,512]{1,0:T(4,128)S(1)}) fusion(f32[512,512]{1,0:T(8,128)S(1)} %get-tuple-element.221, f32[3,512]{1,0:T(4,128)S(1)} %get-tuple-element.216, f32[3,512]{1,0:T(4,128)S(1)} %get-tuple-element.217, f32[512,512]{1,0:T(8,128)S(1)} %get-tuple-element.222, f32[3,512]{1,0:T(4,128)S(1)} %get-tuple-element.214, ...), kind=kLoop, calls=%fused_computation.9.clone.1 | loop fusion | flops 6288384 | bytes 2134016 | tf_op jit(solution)/shard_map/while/body/eval_jaxpr/while/body/eval_jaxpr/reduce_sum | solution.py:30
  64.4 1.0 %fusion.13 = (f32[512,512]{1,0:T(8,128)S(1)}, f32[512,512]{1,0:T(8,128)S(1)}) fusion(f32[3,512]{1,0:T(4,128)S(1)} %get-tuple-element.214, f32[3,512]{1,0:T(4,128)S(1)} %get-tuple-element.215, f32[3,512]{1,0:T(4,128)S(1)} %get-tuple-element.216, f32[3,512]{1,0:T(4,128)S(1)} %get-tuple-element.217), kind=kLoop, calls=%fused_computation.10.clone.1 | loop fusion | flops 4194304 | bytes 2121728 | tf_op jit(solution)/shard_map/while/body/eval_jaxpr/while/body/eval_jaxpr/reduce_sum | solution.py:29
  65.4 0.3 multiply_multiply_fusion.5
  65.7 1.1 %fusion.14 = (f32[3,512]{1,0:T(4,128)S(1)}, f32[3,512]{1,0:T(4,128)S(1)}) fusion(f32[512,512]{1,0:T(8,128)S(1)} %get-tuple-element.221, f32[3,512]{1,0:T(4,128)S(1)} %get-tuple-element.216, f32[3,512]{1,0:T(4,128)S(1)} %get-tuple-element.217, f32[512,512]{1,0:T(8,128)S(1)} %get-tuple-element.222, f32[3,512]{1,0:T(4,128)S(1)} %get-tuple-element.214, ...), kind=kLoop, calls=%fused_computation.9.clone.1 | loop fusion | flops 6288384 | bytes 2134016 | tf_op jit(solution)/shard_map/while/body/eval_jaxpr/while/body/eval_jaxpr/reduce_sum | solution.py:30
  66.9 1.5 %collective-permute-start = (f32[7,1536]{1,0:T(8,128)S(1)}, f32[7,1536]{1,0:T(8,128)S(1)}, u32[]{:S(2)}, u32[]{:S(2)}) collective-permute-start(f32[7,1536]{1,0:T(8,128)S(1)} %bitcast.36), channel_id=1, source_target_pairs={{0,4},{4,0},{8,12},{12,8},{1,5},{5,1},{9,13},{13,9},{2,6},{6,2},{1... | collective-permute-start | bytes 129032 | tf_op jit(solution)/shard_map/ppermute | solution.py:93
  68.4 2.7 %collective-permute-done = f32[7,1536]{1,0:T(8,128)S(1)} collective-permute-done((f32[7,1536]{1,0:T(8,128)S(1)}, f32[7,1536]{1,0:T(8,128)S(1)}, u32[]{:S(2)}, u32[]{:S(2)}) %collective-permute-start) | collective-permute-done | bytes 43040 | tf_op jit(solution)/shard_map/ppermute | solution.py:93
  71.0 2.6 %collective-permute-start.1 = (f32[7,1536]{1,0:T(8,128)S(1)}, f32[7,1536]{1,0:T(8,128)S(1)}, u32[]{:S(2)}, u32[]{:S(2)}) collective-permute-start(f32[7,1536]{1,0:T(8,128)S(1)} %add.78), channel_id=1, source_target_pairs={{0,8},{4,12},{8,0},{12,4},{1,9},{5,13},{9,1},{13,5},{2,10},{6,14},... | collective-permute-start | bytes 129032 | tf_op jit(solution)/shard_map/ppermute | solution.py:93
  73.6 0.0 copy-done
  73.6 0.1 multiply_reduce_fusion.3
  73.7 2.4 %collective-permute-done.1 = f32[7,1536]{1,0:T(8,128)S(1)} collective-permute-done((f32[7,1536]{1,0:T(8,128)S(1)}, f32[7,1536]{1,0:T(8,128)S(1)}, u32[]{:S(2)}, u32[]{:S(2)}) %collective-permute-start.1) | collective-permute-done | bytes 43040 | tf_op jit(solution)/shard_map/ppermute | solution.py:93
  76.1 0.1 fusion.6
  76.2 0.6 pad_maximum_fusion.1
  76.8 0.0 copy-done.1
  (49 shorter events, 0.4 us)
Async XLA Ops:
  7.2 43.7 %all-reduce.2.cloned.1.call-start = ((), (), s32[]{:S(2)}) async-start(), calls=%async_computation | async-start | bytes 196608 | tf_op jit(solution)/shard_map/psum | solution.py:88
  9.1 3.7 %copy-start.2 = (s32[1536]{0:T(1024)S(1)}, s32[1536]{0:T(1024)}, u32[]{:S(2)}) copy-start(s32[1536]{0:T(1024)} %param.14) | copy-start | bytes 18436
  9.1 3.7 %copy-start.3 = (s32[1536]{0:T(1024)S(1)}, s32[1536]{0:T(1024)}, u32[]{:S(2)}) copy-start(s32[1536]{0:T(1024)} %param.15) | copy-start | bytes 18436
  9.9 3.6 %copy-start.4 = (f32[1024]{0:T(1024)S(1)}, f32[1024]{0:T(1024)}, u32[]{:S(2)}) copy-start(f32[1024]{0:T(1024)} %param.12) | copy-start | bytes 12292
  51.6 22.0 %copy-start = (f32[13,1536]{1,0:T(8,128)S(1)}, f32[13,1536]{1,0:T(8,128)}, u32[]{:S(2)}) copy-start(f32[13,1536]{1,0:T(8,128)} %all-reduce.2.cloned.1.call-done) | copy-start | bytes 239620
  66.9 4.2 %collective-permute-start = (f32[7,1536]{1,0:T(8,128)S(1)}, f32[7,1536]{1,0:T(8,128)S(1)}, u32[]{:S(2)}, u32[]{:S(2)}) collective-permute-start(f32[7,1536]{1,0:T(8,128)S(1)} %bitcast.36), channel_id=1, source_target_pairs={{0,4},{4,0},{8,12},{12,8},{1,5},{5,1},{9,13},{13,9},{2,6},{6,2},{1... | collective-permute-start | bytes 129032 | tf_op jit(solution)/shard_map/ppermute | solution.py:93
  71.0 5.0 %collective-permute-start.1 = (f32[7,1536]{1,0:T(8,128)S(1)}, f32[7,1536]{1,0:T(8,128)S(1)}, u32[]{:S(2)}, u32[]{:S(2)}) collective-permute-start(f32[7,1536]{1,0:T(8,128)S(1)} %add.78), channel_id=1, source_target_pairs={{0,8},{4,12},{8,0},{12,4},{1,9},{5,13},{9,1},{13,5},{2,10},{6,14},... | collective-permute-start | bytes 129032 | tf_op jit(solution)/shard_map/ppermute | solution.py:93
  76.1 0.7 copy-start.1
Sparse Core Ops, SparseCore 0:
  13.6 37.1 all-reduce.1
